TPU v7x, 256 devices: a whole 4x4x8 slice. The times are simulated.
256 devices in a mesh: seq: 32 (over y, z), head: 8 (over x, core).
Axes of the slice: x: 4, y: 4, z: 8, core: 2. Of those that a mesh axis runs over, the one named last changes fastest.
Arguments:
- queries: bfloat16 [8192, 32, 128], P('seq', 'head'), may hold values from -42 to 42, as said below
- keys: bfloat16 [8192, 8, 128], P('seq', 'head'), may hold values from -6 to 6
- values: bfloat16 [8192, 8, 128], P('seq', 'head'), may hold values from -6 to 6
- feat_q: bfloat16 [32, 128, 128], P('head'), may hold values from -0.5 to 0.5
- feat_k: bfloat16 [32, 128, 128], P('head'), may hold values from -0.5 to 0.5
- samples: int32 [32], replicated, may hold values from 0 to 1
Outputs:
- student: bfloat16 [8192, 32, 128], P('seq', 'head')
- teacher: float32 [32, 128, 32, 128], P('seq', None, 'head')
- loss: float32 [], replicated
Inputs may be any that keep to these rules, and one draw needn't show every extreme that they name: `queries`: query vectors; some may be large multiples of earlier key vectors.
All inputs are finite; a program needn't handle non-finite values.
Results may differ from a plain program's by a relative error of at most 0.009.
Values may be sent and summed in bfloat16 or wider, within the bound.
No kernel may reach another device: no remote copies, remote signals or barrier semaphores. Data moves between devices by JAX's collectives and lax.ppermute only.
A program may use at most 64 MiB of HBM per device.

v0:
```python
import jax
import jax.numpy as jnp
from jax import lax
from jax.sharding import PartitionSpec as P

HD = 128
FEAT = 128
QH_DEV = 4
BLOCK = 128
PRECISE = lax.Precision.HIGHEST
MASKED = -1e30


def prefix(x, axis, combine, identity):
    count, mine = (lax.axis_size(axis), lax.axis_index(axis))
    everything = jax.tree.map(
        lambda part, kind: lax.all_gather(part.astype(kind), axis), x, (jnp.bfloat16, jnp.bfloat16)
    )
    start = jax.tree.map(
        lambda part, zero: jnp.broadcast_to(jnp.asarray(zero, part.dtype), part.shape), x, identity
    )

    def lap(k, before):
        reached = k < mine
        new = combine(
            before, jax.tree.map(lambda part, own: part[k].astype(own.dtype), everything, x)
        )
        return jax.tree.map(lambda a, b: jnp.where(reached, a, b), new, before)

    return lax.fori_loop(0, count, lap, start)


def features(logits):
    return jnp.concatenate(
        [jax.nn.softmax(logits, axis=-1), jax.nn.softmax(-logits, axis=-1)], axis=-1
    ).astype(jnp.bfloat16)


def add_pair(earlier, later):
    return (earlier[0] + later[0], earlier[1] + later[1])


def absorb(running, query_rows, row_places, key_part, value_part, inv_root):
    best, totals, accum = running
    scores = (
        jnp.einsum("bhd,kd->hbk", query_rows, key_part, preferred_element_type=jnp.float32)
        * inv_root
    )
    key_places = jnp.arange(key_part.shape[0])
    live = (key_places[None, :] <= row_places[:, None])[None]
    peak = jnp.max(jnp.where(live, scores, MASKED), axis=-1)
    newtop = jnp.maximum(best, peak)
    weights = jnp.where(live, jnp.exp(scores - newtop[..., None]), 0.0)
    totals = jnp.sum(weights, axis=-1)
    accum = jnp.einsum(
        "hbk,kd->hbd", weights.astype(jnp.bfloat16), value_part, preferred_element_type=jnp.float32
    )
    return (newtop, totals, accum)


def on_device(queries, keys, values, feat_q, feat_k, samples):
    tok_rows, head_count, head_width = queries.shape
    stretch_count = lax.axis_size("seq")
    inv_root = 1.0 / head_width**0.5
    key_rows = keys[:, 0]
    value_rows = values[:, 0]
    phi_q = features(
        jnp.einsum("lhd,hdf->lhf", queries, feat_q, preferred_element_type=jnp.float32)
    )
    phi_k = features(
        jnp.einsum("ld,hdf->lhf", key_rows, feat_k, preferred_element_type=jnp.float32)
    )
    span_rows = min(tok_rows, 512)
    block_count = tok_rows // span_rows
    fq_blocks = phi_q.reshape(block_count, span_rows, head_count, 2 * FEAT)
    fk_blocks = phi_k.reshape(block_count, span_rows, head_count, 2 * FEAT)
    value_blocks = value_rows.reshape(block_count, span_rows, head_width)
    block_states = jnp.einsum(
        "nlhf,nld->nhfd", fk_blocks, value_blocks, preferred_element_type=jnp.float32
    )
    block_totals = jnp.sum(fk_blocks, axis=1, dtype=jnp.float32)
    local_state = jnp.sum(block_states, axis=0)
    local_total = jnp.sum(block_totals, axis=0)
    empty_state = jnp.zeros_like(local_state)
    empty_total = jnp.zeros_like(local_total)
    enter_state, enter_total = prefix(
        (local_state, local_total), "seq", add_pair, (empty_state, empty_total)
    )
    before_states = jnp.cumsum(block_states, axis=0) - block_states
    before_totals = jnp.cumsum(block_totals, axis=0) - block_totals
    states_in = enter_state[None] + before_states
    totals_in = enter_total[None] + before_totals
    causal = jnp.arange(span_rows)[:, None] >= jnp.arange(span_rows)[None, :]
    kernel = jnp.einsum("nihf,njhf->nhij", fq_blocks, fk_blocks, preferred_element_type=jnp.float32)
    kernel = jnp.where(causal[None, None], kernel, 0.0)
    kernel_low = kernel.astype(jnp.bfloat16)
    numer = jnp.einsum(
        "nhij,njd->nihd", kernel_low, value_blocks, preferred_element_type=jnp.float32
    )
    numer = numer + jnp.einsum(
        "nihf,nhfd->nihd",
        fq_blocks,
        states_in,
        precision=PRECISE,
        preferred_element_type=jnp.float32,
    )
    denom = jnp.transpose(jnp.sum(kernel, axis=3), (0, 2, 1)) + jnp.einsum(
        "nihf,nhf->nih", fq_blocks, totals_in, precision=PRECISE, preferred_element_type=jnp.float32
    )
    student = (
        (numer / denom[..., None]).astype(jnp.bfloat16).reshape(tok_rows, head_count, head_width)
    )
    device_index = lax.axis_index("seq")
    picked = samples[device_index]
    row_first = device_index * tok_rows + picked * BLOCK
    query_rows = lax.dynamic_slice_in_dim(queries, picked * BLOCK, BLOCK, 0)
    row_places = row_first + jnp.arange(BLOCK)
    fresh = (
        jnp.full((head_count, BLOCK), MASKED, jnp.float32),
        jnp.zeros((head_count, BLOCK), jnp.float32),
        jnp.zeros((head_count, BLOCK, head_width), jnp.float32),
    )
    key_part = lax.all_gather(keys, "seq", axis=0, tiled=True)
    value_part = lax.all_gather(values, "seq", axis=0, tiled=True)
    best, totals, accum = lax.cond(
        jnp.int32(0) <= row_first + BLOCK - 1,
        lambda kept: absorb(
            kept, query_rows, row_places, key_part[:, 0], value_part[:, 0], inv_root
        ),
        lambda kept: kept,
        fresh,
    )
    mixed = accum / totals[..., None]
    teacher = jnp.transpose(mixed, (1, 0, 2))[None]
    student_rows = lax.dynamic_slice_in_dim(student, picked * BLOCK, BLOCK, 0).astype(jnp.float32)
    gap = student_rows - teacher[0]
    entry_count = stretch_count * lax.axis_size("head") * BLOCK * QH_DEV * HD
    loss = lax.psum(jnp.sum(gap * gap), ("seq", "head")) / entry_count
    return (student, teacher, loss)


def solution(mesh):
    in_specs = (
        P("seq", "head", None),
        P("seq", "head", None),
        P("seq", "head", None),
        P("head", None, None),
        P("head", None, None),
        P(),
    )
    out_specs = (P("seq", "head", None), P("seq", None, "head", None), P())
    return jax.shard_map(
        on_device, mesh=mesh, in_specs=in_specs, out_specs=out_specs, check_vma=False
    )
```

profile of v0, /device:TPU:1, one launch (start us, length us, event | category | flops | bytes accessed | tf_op | source)
XLA Modules:
  0.0 396.0 jit_solution(10727178128986259759)
XLA Ops:
  12.6 1.8 fusion.65
  14.5 1.3 dynamic_slice.26
  16.7 42.3 %all-gather.2 = bf16[32,4,256]{2,1,0:T(4,128)(2,1)S(1)} all-gather(bf16[1,4,256]{2,1,0:T(4,128)(2,1)S(1)} %convert_bitcast_fusion), channel_id=3, replica_groups=mesh['seq'=32,'head'=8] {'seq'}, dimensions={0}, use_global_device_ids=true | all-gather | bytes 67584 | tf_op jit(solution)/shard_map/all_gather | solution.py:17
  59.1 1.3 fusion.66
  60.4 1.3 fusion.69
  62.2 25.6 %all-gather.7.cloned.1.call-done = bf16[8192,1,128]{2,0,1:T(8,128)(2,1)} async-done(((bf16[256,1,128]{2,0,1:T(8,128)(2,1)}), bf16[8192,1,128]{2,0,1:T(8,128)(2,1)}) %all-gather.7.cloned.1.call-update) | async-done | bytes 2097168 | tf_op jit(solution)/shard_map/all_gather | solution.py:123
  87.8 77.7 %all-gather.9.cloned.1.call-done = bf16[8192,1,128]{2,0,1:T(8,128)(2,1)} async-done(((bf16[256,1,128]{2,0,1:T(8,128)(2,1)}), bf16[8192,1,128]{2,0,1:T(8,128)(2,1)}) %all-gather.9.cloned.1.call-update) | async-done | bytes 2097168 | tf_op jit(solution)/shard_map/all_gather | solution.py:124
  165.5 16.0 %conditional.1 = (f32[4,128]{1,0:T(4,128)S(1)}, f32[4,128,128]{2,1,0:T(8,128)S(1)}) conditional(s32[]{:T(128)} %convert_element_type.94, () %tuple.33, (s32[]{:T(128)}, s32[128]{0:T(128)S(1)}, bf16[256,4,128]{2,1,0:T(4,128)(2,1)}, s32[]{:T(128)}, bf16[8192,1,128]{2,0,1:T(8,128)(2,1)}, /*index=5*/bf16[8192,1,128]{2,0,1:T(8,128)(2,1)}) %tuple.34), branch_computations={%region_12.13_spmd, %region_13.0_spmd} | conditional | flops 2194669056 | bytes 59651608 | solution.py:125
  167.2 4.8 %fusion = (f32[4,128]{1,0:T(4,128)S(1)}, f32[128,4,8192]{2,0,1:T(8,128)S(1)}) fusion(pred[128,8192]{1,0:T(8,128)(4,1)S(1)} %iota_compare_fusion, bf16[8192,1,128]{2,0,1:T(8,128)(2,1)} %get-tuple-element.140, bf16[256,4,128]{2,0,1:T(8,128)(2,1)S(1)} %copy.30, s32[]{:T(128)} %get-tuple-element.139), kind=kOutput, calls=%fused_computation.2 | convolution fusion | flops 1086324224 | bytes 20056068 | tf_op jit(solution)/shard_map/cond/branch_1_fun/bhd,kd->hbk/dot_general | solution.py:46
  172.0 4.8 %fusion.5 = f32[4,128,128]{2,1,0:T(8,128)S(1)} fusion(f32[128,4,8192]{2,0,1:T(8,128)S(1)} %get-tuple-element.205, f32[4,128]{1,0:T(4,128)S(1)} %broadcast_maximum_fusion, pred[128,8192]{1,0:T(8,128)(4,1)S(1)} %iota_compare_fusion, bf16[8192,1,128]{2,0,1:T(8,128)(2,1)} %get-tuple-element.141), kind=kOutput, calls=%fused_computation.7 | convolution fusion | flops 1090519040 | bytes 20187136 | tf_op jit(solution)/shard_map/cond/branch_1_fun/hbk,kd->hbd/dot_general | solution.py:55
  176.8 4.6 %fusion.4 = f32[4,128]{1,0:T(4,128)S(1)} fusion(f32[128,4,8192]{2,0,1:T(8,128)S(1)} %get-tuple-element.205, f32[4,128]{1,0:T(4,128)S(1)} %broadcast_maximum_fusion, pred[128,8192]{1,0:T(8,128)(4,1)S(1)} %iota_compare_fusion), kind=kLoop, calls=%fused_computation.6 | loop fusion | flops 16776704 | bytes 17829888 | tf_op jit(solution)/shard_map/cond/branch_1_fun/reduce_sum | solution.py:54
  181.6 86.1 %all-gather.11.cloned.1.call-done = bf16[128,256,128]{2,1,0:T(8,128)(2,1)} async-done(((bf16[4,256,128]{2,1,0:T(8,128)(2,1)}), bf16[128,256,128]{2,1,0:T(8,128)(2,1)}) %all-gather.11.cloned.1.call-update) | async-done | bytes 8388624 | tf_op jit(solution)/shard_map/all_gather | solution.py:17
  267.6 40.8 %while.16 = (s32[]{:T(128)}, f32[4,256,128]{2,1,0:T(8,128)S(1)}, f32[4,256]{1,0:T(4,128)S(1)}, s32[]{:T(128)}, bf16[32,4,256,128]{3,2,1,0:T(8,128)(2,1)}, /*inde...) while((s32[]{:T(128)}, f32[4,256,128]{2,1,0:T(8,128)S(1)}, f32[4,256]{1,0:T(4,128)S(1)}, ...), condition=%wide.region_10.0_spmd.clone, body=%wide.region_9.0_spmd.clone.sunk | while | flops 528388 | bytes 1321083 | solution.py:30
  268.9 1.2 add_select_fusion.4
  270.2 1.2 add_select_fusion.4
  271.5 1.2 add_select_fusion.4
  272.7 1.2 add_select_fusion.4
  274.0 1.2 add_select_fusion.4
  275.3 1.2 add_select_fusion.4
  276.6 1.2 add_select_fusion.4
  277.8 1.2 add_select_fusion.4
  279.1 1.2 add_select_fusion.4
  280.4 1.2 add_select_fusion.4
  281.7 1.2 add_select_fusion.4
  282.9 1.2 add_select_fusion.4
  284.2 1.2 add_select_fusion.4
  285.5 1.2 add_select_fusion.4
  286.8 1.2 add_select_fusion.4
  288.0 1.2 add_select_fusion.4
  303.4 1.2 add_select_fusion.4
  305.9 1.2 add_select_fusion.4
  311.5 75.3 %psum.7 = f32[]{:T(128)} all-reduce(f32[]{:T(128)} %fusion.37), channel_id=1, replica_groups=mesh['seq'=32,'head'=8] {'seq','head'}, use_global_device_ids=true, to_apply=%region_17.18 | all-reduce | flops 1 | bytes 8 | tf_op jit(solution)/shard_map/psum | solution.py:138
  (82 shorter events, 29.7 us)
Async XLA Ops:
  7.2 51.9 %copy-start = (bf16[4,128,128]{2,1,0:T(8,128)(2,1)S(1)}, bf16[4,128,128]{2,1,0:T(8,128)(2,1)}, u32[]{:S(2)}) copy-start(bf16[4,128,128]{2,1,0:T(8,128)(2,1)} %param.13) | copy-start | bytes 393220
  7.2 80.6 %all-gather.7.cloned.1.call-start = ((), (), s32[]{:S(2)}) async-start(), calls=%async_computation | async-start | bytes 2162688 | tf_op jit(solution)/shard_map/all_gather | solution.py:123
  7.9 157.5 %all-gather.9.cloned.1.call-start = ((), (), s32[]{:S(2)}) async-start(), calls=%async_computation.1 | async-start | bytes 2162688 | tf_op jit(solution)/shard_map/all_gather | solution.py:124
  8.7 259.0 %all-gather.11.cloned.1.call-start = ((), (), s32[]{:S(2)}) async-start(), calls=%async_computation.2 | async-start | bytes 8650752 | tf_op jit(solution)/shard_map/all_gather | solution.py:17
  165.5 144.0 %copy-start.1 = (bf16[256,1,128]{2,0,1:T(8,128)(2,1)S(1)}, bf16[256,1,128]{2,0,1:T(8,128)(2,1)}, u32[]{:S(2)}) copy-start(bf16[256,1,128]{2,0,1:T(8,128)(2,1)} %param.12) | copy-start | bytes 196612
Sparse Core Ops, SparseCore 0:
  10.6 77.1 all-gather.6
  90.4 75.0 all-gather.8
  168.6 98.9 all-gather.10
where the time goes:
time: 397 us; the launch traced here: 396 us
  waiting for transfers between devices  191 us (48%)
  blocking collectives  118 us (30%)
  other arithmetic  47.1 us (12%)
  matrix products  18.1 us (5%)
  between operations  16.4 us (4%)
  local copies, waits for them, and re-layouts  5.16 us (1%)
    all_gather x1, waiting for transfers between devices, prefix(): lax.all_gather(part.astype(kind), axis)  86.1 us
    all_gather x1, waiting for transfers between devices, on_device(): value_part = lax.all_gather(values, 'seq', axis=0, tiled=True)  77.7 us
    psum x1, blocking collectives, on_device(): loss = lax.psum(jnp.sum(gap * gap), ('seq', 'head')) / entry_count  75.3 us
    all_gather x1, blocking collectives, prefix(): lax.all_gather(part.astype(kind), axis)  42.3 us
    select_n x64, other arithmetic, lap(): return jax.tree.map(lambda a, b: jnp.where(reached, a, b), new, before)  40 us
    all_gather x1, waiting for transfers between devices, on_device(): key_part = lax.all_gather(keys, 'seq', axis=0, tiled=True)  25.6 us
  transfers between devices with their start and end apart: 3, of which 3 were waited for; matrix products, arithmetic and copies ran while one was open for 7% of the time, Pallas kernels for 0%

commit v1 on v0

--- a/solution.py
+++ b/solution.py
@@ -121,7 +121,9 @@
         jnp.zeros((head_count, BLOCK, head_width), jnp.float32),
     )
     key_part = lax.all_gather(keys, "seq", axis=0, tiled=True)
-    value_part = lax.all_gather(values, "seq", axis=0, tiled=True)
+    value_part = jnp.concatenate(
+        lax.all_to_all(jnp.stack([values] * lax.axis_size("seq")), "seq", 0, 0), axis=0
+    )
     best, totals, accum = lax.cond(
         jnp.int32(0) <= row_first + BLOCK - 1,
         lambda kept: absorb(

time: 397 us -> 349 us (0.88)
  waiting for transfers between devices: 191 us -> 61.3 us
  blocking collectives: 118 us -> 162 us
  other arithmetic: 47.1 us -> 68.6 us
  starting transfers between devices: 0.11 us -> 12.2 us
    all_gather x1 -> x0, waiting for transfers between devices: 77.7 us -> none  [on_device(): value_part = lax.all_gather(values, 'seq', axis=0, tiled=True)]
    all_gather x1, blocking collectives: 42.3 us -> 86.4 us  [prefix(): lax.all_gather(part.astype(kind), axis)]
    all_gather x1, waiting for transfers between devices: 25.6 us -> 0.02 us  [on_device(): key_part = lax.all_gather(keys, 'seq', axis=0, tiled=True)]
    all_gather x1, waiting for transfers between devices: 86.1 us -> 60.6 us  [prefix(): lax.all_gather(part.astype(kind), axis)]
    select_n x64, other arithmetic: 40 us -> 61 us  [lap(): return jax.tree.map(lambda a, b: jnp.where(reached, a, b), new, before)]
    all_to_all x0 -> x1, starting transfers between devices: none -> 12.2 us  [on_device(): lax.all_to_all(jnp.stack([values] * lax.axis_size('seq')), 'seq', 0, 0)]
  transfers between devices with their start and end apart: 3 -> 3, of which waited for: 3 -> 1; matrix products, arithmetic and copies ran while one was open for 7% -> 8% of each run, Pallas kernels for 0% -> 0%
where the time goes in v1:
time: 349 us; the launch traced here: 346 us
  blocking collectives  162 us (46%)
  other arithmetic  68.6 us (20%)
  waiting for transfers between devices  61.3 us (18%)
  matrix products  18.8 us (5%)
  between operations  16.7 us (5%)
  starting transfers between devices  12.2 us (3%)
  local copies, waits for them, and re-layouts  6.78 us (2%)
    all_gather x1, blocking collectives, prefix(): lax.all_gather(part.astype(kind), axis)  86.4 us
    psum x1, blocking collectives, on_device(): loss = lax.psum(jnp.sum(gap * gap), ('seq', 'head')) / entry_count  75.3 us
    select_n x64, other arithmetic, lap(): return jax.tree.map(lambda a, b: jnp.where(reached, a, b), new, before)  61 us
    all_gather x1, waiting for transfers between devices, prefix(): lax.all_gather(part.astype(kind), axis)  60.6 us
    all_to_all x1, starting transfers between devices, on_device(): lax.all_to_all(jnp.stack([values] * lax.axis_size('seq')), 'seq', 0, 0)  12.2 us
  transfers between devices with their start and end apart: 3, of which 1 were waited for; matrix products, arithmetic and copies ran while one was open for 8% of the time, Pallas kernels for 0%

profile of v1, /device:TPU:1, one launch (start us, length us, event | category | flops | bytes accessed | tf_op | source)
XLA Modules:
  0.0 346.4 jit_solution(10392515710061401308)
XLA Ops:
  11.9 1.8 fusion.64
  13.7 2.7 stack.2
  16.4 12.2 %all-to-all-start = ((bf16[32,256,1,128]{3,1,2,0:T(8,128)(2,1)}), bf16[32,256,1,128]{3,1,2,0:T(8,128)(2,1)}, u32[]{:S(2)}, u32[]{:S(2)}) async-start(bf16[32,256,1,128]{3,1,2,0:T(8,128)(2,1)} %stack.2), calls=%async_computation | async-start | bytes 4194304 | tf_op jit(solution)/shard_map/all_to_all | solution.py:125
  28.6 1.2 dynamic_slice.26
  30.7 86.4 %all-gather.2 = bf16[32,4,256]{2,1,0:T(4,128)(2,1)} all-gather(bf16[1,4,256]{2,1,0:T(4,128)(2,1)S(1)} %convert_bitcast_fusion), channel_id=3, replica_groups=mesh['seq'=32,'head'=8] {'seq'}, dimensions={0}, use_global_device_ids=true | all-gather | bytes 67584 | tf_op jit(solution)/shard_map/all_gather | solution.py:17
  117.8 1.3 fusion.65
  119.2 1.3 fusion.68
  121.9 14.9 %conditional.1 = (f32[4,128]{1,0:T(4,128)S(1)}, f32[4,128,128]{2,1,0:T(8,128)S(1)}) conditional(s32[]{:T(128)} %convert_element_type.94, () %tuple.33, (s32[]{:T(128)}, s32[128]{0:T(128)S(1)}, bf16[256,4,128]{2,1,0:T(4,128)(2,1)S(1)}, s32[]{:T(128)}, bf16[8192,1,128]{2,0,1:T(8,128)(2,1)}, /*index=5*/bf16[32,256,1,128]{3,1,2,0:T(8,128)(2,1)}) %tuple.71), branch_computations={%region_12.13_spmd, %region_13.0_spmd} | conditional | flops 2194669056 | bytes 59651608 | solution.py:127
  122.6 4.8 %fusion = (f32[4,128]{1,0:T(4,128)S(1)}, f32[128,4,8192]{2,0,1:T(8,128)S(1)}) fusion(pred[128,8192]{1,0:T(8,128)(4,1)S(1)} %iota_compare_fusion, bf16[8192,1,128]{2,0,1:T(8,128)(2,1)} %get-tuple-element.140, bf16[256,4,128]{2,0,1:T(8,128)(2,1)S(1)} %copy.30, s32[]{:T(128)} %get-tuple-element.139), kind=kOutput, calls=%fused_computation.2 | convolution fusion | flops 1086324224 | bytes 20056068 | tf_op jit(solution)/shard_map/cond/branch_1_fun/bhd,kd->hbk/dot_general | solution.py:46
  127.4 4.7 %fusion.5 = f32[4,128,128]{2,1,0:T(8,128)S(1)} fusion(bf16[8192,128,1]{1,0,2:T(8,128)(2,1)} %bitcast.5, f32[128,4,8192]{2,0,1:T(8,128)S(1)} %get-tuple-element.205, f32[4,128]{1,0:T(4,128)S(1)} %broadcast_maximum_fusion, pred[128,8192]{1,0:T(8,128)(4,1)S(1)} %iota_compare_fusion), kind=kOutput, calls=%fused_computation.7 | convolution fusion | flops 1090519040 | bytes 20187136 | tf_op jit(solution)/shard_map/cond/branch_1_fun/hbk,kd->hbd/dot_general | solution.py:55
  132.1 4.5 %fusion.4 = f32[4,128]{1,0:T(4,128)S(1)} fusion(f32[128,4,8192]{2,0,1:T(8,128)S(1)} %get-tuple-element.205, f32[4,128]{1,0:T(4,128)S(1)} %broadcast_maximum_fusion, pred[128,8192]{1,0:T(8,128)(4,1)S(1)} %iota_compare_fusion), kind=kLoop, calls=%fused_computation.6 | loop fusion | flops 16776704 | bytes 17829888 | tf_op jit(solution)/shard_map/cond/branch_1_fun/reduce_sum | solution.py:54
  137.0 60.6 %all-gather.8.cloned.1.call-done = bf16[128,256,128]{2,1,0:T(8,128)(2,1)} async-done(((bf16[4,256,128]{2,1,0:T(8,128)(2,1)}), bf16[128,256,128]{2,1,0:T(8,128)(2,1)}) %all-gather.8.cloned.1.call-update) | async-done | bytes 8388624 | tf_op jit(solution)/shard_map/all_gather | solution.py:17
  197.6 61.0 %while.16 = (s32[]{:T(128)}, f32[4,256,128]{2,1,0:T(8,128)S(1)}, f32[4,256]{1,0:T(4,128)S(1)}, s32[]{:T(128)}, bf16[32,4,256,128]{3,2,1,0:T(8,128)(2,1)}, /*index=5*/bf16[32,4,256]{2,1,0:T(4,128)(2,1)}, s32[]{:T(128)}, s32[]{:T(128)}) while((s32[]{:T(128)}, f32[4,256,128]{2,1,0:T(8,128)S(1)}, f32[4,256]{1,0:T(4,128)S(1)}, ...), condition=%wide.region_10.0_spmd.clone, body=%wide.region_9.0_spmd.clone.sunk | while | flops 528388 | bytes 1321075 | solution.py:30
  197.6 1.2 add_select_fusion.4
  199.5 1.2 add_select_fusion.4
  201.4 1.2 add_select_fusion.4
  203.3 1.2 add_select_fusion.4
  205.2 1.2 add_select_fusion.4
  207.1 1.2 add_select_fusion.4
  209.0 1.2 add_select_fusion.4
  210.9 1.2 add_select_fusion.4
  212.8 1.2 add_select_fusion.4
  214.7 1.2 add_select_fusion.4
  216.6 1.2 add_select_fusion.4
  218.5 1.2 add_select_fusion.4
  220.4 1.2 add_select_fusion.4
  222.3 1.2 add_select_fusion.4
  224.2 1.2 add_select_fusion.4
  226.1 1.2 add_select_fusion.4
  228.1 1.2 add_select_fusion.4
  239.5 1.2 add_select_fusion.4
  261.6 75.3 %psum.7 = f32[]{:T(128)} all-reduce(f32[]{:T(128)} %fusion.36), channel_id=1, replica_groups=mesh['seq'=32,'head'=8] {'seq','head'}, use_global_device_ids=true, to_apply=%region_17.18 | all-reduce | flops 1 | bytes 8 | tf_op jit(solution)/shard_map/psum | solution.py:140
  (84 shorter events, 50.5 us)
Async XLA Ops:
  7.2 110.7 %copy-start = (bf16[4,128,128]{2,1,0:T(8,128)(2,1)S(1)}, bf16[4,128,128]{2,1,0:T(8,128)(2,1)}, u32[]{:S(2)}) copy-start(bf16[4,128,128]{2,1,0:T(8,128)(2,1)} %param.13) | copy-start | bytes 393220
  7.2 114.7 %copy-start.1 = (bf16[256,4,128]{2,1,0:T(4,128)(2,1)S(1)}, bf16[256,4,128]{2,1,0:T(4,128)(2,1)}, u32[]{:S(2)}) copy-start(bf16[256,4,128]{2,1,0:T(4,128)(2,1)} %param.10) | copy-start | bytes 786436
  7.2 114.6 %all-gather.6.cloned.1.call-start = ((), (), s32[]{:S(2)}) async-start(), calls=%async_computation.1 | async-start | bytes 2162688 | tf_op jit(solution)/shard_map/all_gather | solution.py:123
  7.9 189.6 %all-gather.8.cloned.1.call-start = ((), (), s32[]{:S(2)}) async-start(), calls=%async_computation.2 | async-start | bytes 8650752 | tf_op jit(solution)/shard_map/all_gather | solution.py:17
  16.4 105.4 %all-to-all-start = ((bf16[32,256,1,128]{3,1,2,0:T(8,128)(2,1)}), bf16[32,256,1,128]{3,1,2,0:T(8,128)(2,1)}, u32[]{:S(2)}, u32[]{:S(2)}) async-start(bf16[32,256,1,128]{3,1,2,0:T(8,128)(2,1)} %stack.2), calls=%async_computation | async-start | bytes 4194304 | tf_op jit(solution)/shard_map/all_to_all | solution.py:125
  121.9 137.8 %copy-start.2 = (bf16[256,1,128]{2,0,1:T(8,128)(2,1)S(1)}, bf16[256,1,128]{2,0,1:T(8,128)(2,1)}, u32[]{:S(2)}) copy-start(bf16[256,1,128]{2,0,1:T(8,128)(2,1)} %param.12) | copy-start | bytes 196612
Sparse Core Ops, SparseCore 0:
  10.6 84.9 all-gather.5
  98.8 98.7 all-gather.7
